TPU v7x, 256 devices: a whole 4x4x8 slice. The times are simulated.
256 devices in a mesh: grp: 8 (over z), tp: 32 (over x, y, core).
Axes of the slice: x: 4, y: 4, z: 8, core: 2. Of those that a mesh axis runs over, the one named last changes fastest.
Arguments:
- hidden: bfloat16 [8192, 20480], P('grp', 'tp'), may hold values from -6 to 6
- down_weight: bfloat16 [20480, 8192], P('tp'), may hold values from -0.078125 to 0.078125
- adapter_down_factor: bfloat16 [64, 64, 20480], P('grp', None, 'tp'), may hold values from -0.0390625 to 0.0390625
- adapter_up_factor: bfloat16 [64, 64, 8192], P('grp', None, 'tp'), may hold values from -0.75 to 0.75
- row_tile_adapter: int32 [64], P('grp'), may hold values from 0 to 63, as said below
- adapter_pool_slot: int32 [64], replicated, may hold values from 0 to 63, as said below
Outputs:
- output: bfloat16 [8192, 8192], P('grp', 'tp')
Inputs may be any that keep to these rules, and one draw needn't show every extreme that they name: adapter_pool_slot is a permutation; slot s of the pool is held by group s // 8. `row_tile_adapter`: at most 4 tiles of one group have adapters held by one owner group, and in every draw one owner group holds the adapters of exactly 4 tiles of every group.
All inputs are finite; a program needn't handle non-finite values.
Results may differ from a plain program's by a relative error of at most 0.019.
Values may be sent and summed in bfloat16 or wider, within the bound.
A program may use at most 128 MiB of HBM per device.

v0:
```python
import jax
import jax.numpy as jnp
from jax import lax
from jax.sharding import PartitionSpec as P

adapter_scale = 2.0


def local(
    hidden, down_weight, adapter_down_factor, adapter_up_factor, row_tile_adapter, adapter_pool_slot
):
    tok_rows, feat_cols = hidden.shape
    tile_count = row_tile_adapter.shape[0]
    tile_rows = tok_rows // tile_count
    slot_table = adapter_pool_slot[row_tile_adapter]
    base_cols = lax.psum_scatter(
        lax.dot_general(
            down_weight, hidden, (((0,), (1,)), ((), ())), preferred_element_type=jnp.float32
        ).astype(jnp.bfloat16),
        "tp",
        scatter_dimension=0,
        tiled=True,
    ).astype(jnp.float32)
    pooled_down, pooled_up = (
        lax.all_gather(adapter_down_factor, "grp", axis=0, tiled=True),
        lax.all_gather(adapter_up_factor, "grp", axis=0, tiled=True),
    )
    tile_blocks = hidden.reshape(tile_count, tile_rows, feat_cols)
    rank_part = jnp.einsum(
        "ktf,krf->ktr", tile_blocks, pooled_down[slot_table], preferred_element_type=jnp.float32
    )
    rank_projections = lax.psum(rank_part.astype(jnp.bfloat16), "tp")
    adapted_output = (
        jnp.einsum(
            "pjf,pfb->pjb",
            rank_projections,
            pooled_up[slot_table],
            preferred_element_type=jnp.float32,
        )
        * adapter_scale
    ).astype(jnp.bfloat16)
    adapter_delta = adapted_output.reshape(tok_rows, -1).astype(jnp.float32)
    return (base_cols.T + adapter_delta).astype(jnp.bfloat16)


def solution(mesh):
    placed = (
        P("grp", "tp"),
        P("tp", None),
        P("grp", None, "tp"),
        P("grp", None, "tp"),
        P("grp"),
        P(),
    )
    return jax.shard_map(
        local, mesh=mesh, in_specs=placed, out_specs=P("grp", "tp"), check_vma=False
    )
```

profile of v0, /device:TPU:1, one launch (start us, length us, event | category | flops | bytes accessed | tf_op | source)
XLA Modules:
  0.0 366.1 jit_solution(15145106554480718428)
XLA Ops:
  6.5 0.0 copy-start
  6.5 0.0 all-gather.3.cloned.1.call-start
  6.5 0.7 all-gather.3.cloned.1.call-update
  7.3 0.0 all-gather.5.cloned.1.call-start
  7.3 0.7 all-gather.5.cloned.1.call-update
  8.0 0.0 all-reduce.2.cloned.1.call-start
  8.1 0.7 compare_select_fusion.1
  8.7 1.3 gather_fusion
  10.0 67.3 %all-gather.3.cloned.1.call-done = bf16[64,64,640]{2,1,0:T(8,128)(2,1)} async-done(((bf16[8,64,640]{2,1,0:T(8,128)(2,1)}), bf16[64,64,640]{2,1,0:T(8,128)(2,1)}) %all-gather.3.cloned.1.call-update) | async-done | bytes 5242896 | tf_op jit(solution)/shard_map/all_gather | solution.py:25
  77.4 3.1 gather_fusion.1
  80.5 0.0 copy-done
  80.5 1.3 fusion.1
  81.8 0.0 all-reduce.2.cloned.1.call-update
  81.8 0.0 reduce-scatter.2.cloned.1.call-start
  81.9 20.1 %convolution_convert_fusion = bf16[8192,1024]{1,0:T(8,128)(2,1)} fusion(bf16[640,8192]{1,0:T(8,128)(2,1)} %param.7, bf16[1024,640]{1,0:T(8,128)(2,1)S(1)} %copy-done), kind=kOutput, calls=%fused_computation.3 | convolution fusion | flops 10745806848 | bytes 28573696 | tf_op jit(solution)/shard_map/dot_general | solution.py:17
  102.0 0.0 reduce-scatter.2.cloned.1.call-update
  102.0 12.6 %all-gather.5.cloned.1.call-done = bf16[64,64,256]{2,1,0:T(8,128)(2,1)} async-done(((bf16[8,64,256]{2,1,0:T(8,128)(2,1)}), bf16[64,64,256]{2,1,0:T(8,128)(2,1)}) %all-gather.5.cloned.1.call-update) | async-done | bytes 2097168 | tf_op jit(solution)/shard_map/all_gather | solution.py:26
  114.6 2.2 gather_fusion.2
  116.8 115.1 %all-reduce.2.cloned.1.call-done = bf16[8,128,64]{1,2,0:T(8,128)(2,1)} async-done(((bf16[8,128,64]{1,2,0:T(8,128)(2,1)}), bf16[8,128,64]{1,2,0:T(8,128)(2,1)}) %all-reduce.2.cloned.1.call-update) | async-done | bytes 131088 | tf_op jit(solution)/shard_map/psum | solution.py:32
  231.9 1.2 fusion
  233.2 0.1 bitcast_convert_fusion
  233.3 0.3 copy.13
  233.6 123.7 %reduce-scatter.2.cloned.1.call-done = bf16[256,1024]{1,0:T(8,128)(2,1)} async-done(((bf16[8192,1024]{1,0:T(8,128)(2,1)}), bf16[256,1024]{1,0:T(8,128)(2,1)}) %reduce-scatter.2.cloned.1.call-update) | async-done | bytes 524304 | tf_op jit(solution)/shard_map/reduce_scatter | solution.py:16
  357.4 1.2 fusion.2
  358.5 1.0 copy.12
  (3 shorter events, 0.0 us)
Async XLA Ops:
  6.5 74.0 %copy-start = (bf16[1024,640]{1,0:T(8,128)(2,1)S(1)}, bf16[1024,640]{1,0:T(8,128)(2,1)}, u32[]{:S(2)}) copy-start(bf16[1024,640]{1,0:T(8,128)(2,1)} %param.6) | copy-start | bytes 3932164
  6.5 70.8 %all-gather.3.cloned.1.call-start = ((), (), s32[]{:S(2)}) async-start(), calls=%async_computation.2 | async-start | bytes 5898240 | tf_op jit(solution)/shard_map/all_gather | solution.py:25
  7.3 107.4 %all-gather.5.cloned.1.call-start = ((), (), s32[]{:S(2)}) async-start(), calls=%async_computation.4 | async-start | bytes 2359296 | tf_op jit(solution)/shard_map/all_gather | solution.py:26
  8.0 223.9 %all-reduce.2.cloned.1.call-start = ((), (), s32[]{:S(2)}) async-start(), calls=%async_computation.3 | async-start | bytes 262144 | tf_op jit(solution)/shard_map/psum | solution.py:32
  81.8 275.5 %reduce-scatter.2.cloned.1.call-start = ((), (), s32[]{:S(2)}) async-start(), calls=%async_computation.1 | async-start | bytes 17301504 | tf_op jit(solution)/shard_map/reduce_scatter | solution.py:16
Sparse Core Ops, SparseCore 0:
  9.1 68.1 all-gather.2
  79.1 35.4 all-gather.4
  117.8 114.0 all-reduce.1
  236.0 121.3 reduce-scatter.1
where the time goes:
time: 367 us; the launch traced here: 366 us
  waiting for transfers between devices  320 us (87%)
  matrix products  22.6 us (6%)
  between operations  13.2 us (4%)
  local copies, waits for them, and re-layouts  7.93 us (2%)
    reduce_scatter x1, waiting for transfers between devices, local(): lax.psum_scatter(lax.dot_general(down_weight, hidden, (((0,), (1,)), ((),...  124 us
    psum x1, waiting for transfers between devices, local(): rank_projections = lax.psum(rank_part.astype(jnp.bfloat16), 'tp')  115 us
    all_gather x1, waiting for transfers between devices, local(): lax.all_gather(adapter_down_factor, 'grp', axis=0, tiled=True)  67.3 us
    dot_general x1, matrix products, local(): lax.dot_general(down_weight, hidden, (((0,), (1,)), ((), ())), preferred_...  20.1 us
    all_gather x1, waiting for transfers between devices, local(): lax.all_gather(adapter_up_factor, 'grp', axis=0, tiled=True)  12.6 us
  transfers between devices with their start and end apart: 4, of which 4 were waited for; matrix products, arithmetic and copies ran while one was open for 8% of the time, Pallas kernels for 0%

commit v1 on v0

v1 whole, which is shorter than its diff:
```python
import jax
import jax.numpy as jnp
from jax import lax
from jax.experimental import pallas as pl
from jax.experimental.pallas import tpu as pltpu
from jax.sharding import PartitionSpec as P

adapter_scale = 2.0
MESH = pl.DeviceIdType.MESH
NX, NY, NZ, NTP = 4, 4, 8, 32
BF, F32 = jnp.bfloat16, jnp.float32
BLOCK_ORDER = (
    (2, 2), (2, 1), (1, 2), (2, 3), (3, 2), (2, 0), (0, 2), (1, 1),
    (1, 3), (3, 1), (3, 3), (1, 0), (3, 0), (0, 1), (0, 3), (0, 0),
)


def kernel(
    hid, wgt, down, up, tiles, slots, out,
    h_own, h_sib, w_own, w_sib, send1, recv1, send2, recv2, part, hold,
    p_down, s_down, a_down, p_up, s_up, a_up, slot_out, slot_in, slot_s,
    rank_out, rank_in, rank_sum, rank_all,
    l_sem, hs_s, hs_r, ws_s, ws_r, s1_s, s1_r, s2_s, s2_r,
    zs_s, zs_r, zd1_s, zd1_r, zu1_s, zu1_r, zd2_s, zd2_r, zu2_s, zu2_r,
    ra_s, ra_r, rb_s, rb_r, loc_sem,
):
    z = lax.axis_index("grp")
    t = lax.axis_index("tp")
    core = lax.rem(t, 2)
    y = lax.rem(t // 2, NY)
    x = t // (2 * NY)

    def at(xx, yy, cc):
        return {"grp": z, "tp": (lax.rem(xx, NX) * NY + lax.rem(yy, NY)) * 2 + cc}

    def at_z(zz):
        return {"grp": zz, "tp": t}

    def at_t(tt):
        return {"grp": z, "tp": tt}

    def remote(src, dst, ssem, rsem, dev):
        return pltpu.make_async_remote_copy(
            src_ref=src, dst_ref=dst, send_sem=ssem, recv_sem=rsem,
            device_id=dev, device_id_type=MESH,
        )

    sib = at(x, y, 1 - core)

    def load_h(q):
        r = pl.ds(q * 256, 256)
        return pltpu.make_async_copy(hid.at[r], h_own.at[r], l_sem.at[q])

    def blk(ox, oy):
        return lax.rem(x + ox, NX) * NY + lax.rem(y + oy, NY)

    def load_w(b):
        c = pl.multiple_of((2 * b + core) * 256, 256)
        return pltpu.make_async_copy(wgt.at[:, pl.ds(c, 256)], w_own.at[b], l_sem.at[4 + b])

    def swap_h(q):
        r = pl.ds(q * 256, 256)
        return remote(hid.at[r], h_sib.at[r], hs_s.at[q], hs_r.at[q], sib)

    def swap_w(b):
        c = pl.multiple_of((2 * b + 1 - core) * 256, 256)
        return remote(wgt.at[:, pl.ds(c, 256)], w_sib.at[b], ws_s.at[b], ws_r.at[b], sib)

    for q in range(4):
        load_h(q).start()
    for ox, oy in BLOCK_ORDER:
        load_w(blk(ox, oy)).start()
    own_down = pltpu.make_async_copy(down.at[:, z], p_down.at[pl.ds(z * 8, 8)], loc_sem.at[0])
    own_up = pltpu.make_async_copy(up.at[:, z], p_up.at[pl.ds(z * 8, 8)], loc_sem.at[1])
    own_down.start()
    own_up.start()

    row = lax.broadcasted_iota(jnp.int32, (8, 128), 0)
    mine = jnp.zeros((8, 128), jnp.int32)
    for i in range(8):
        mine = jnp.where(row == i, slots[tiles[i]], mine)
    slot_out[...] = mine

    barrier = pltpu.get_barrier_semaphore()

    def greet_t(i, _):
        pl.semaphore_signal(barrier, inc=1, device_id=at_t(lax.rem(t + i, NTP)), device_id_type=MESH)
        return 0

    def greet_z(i, _):
        pl.semaphore_signal(barrier, inc=1, device_id=at_z(lax.rem(z + i, NZ)), device_id_type=MESH)
        return 0

    lax.fori_loop(1, NZ, greet_z, 0)
    lax.fori_loop(1, NTP, greet_t, 0)
    pl.semaphore_wait(barrier, NTP - 1 + NZ - 1)

    def z_slot(p):
        return remote(slot_out, slot_in.at[z], zs_s.at[p], zs_r.at[z], at_z(p))

    def z_down1(p):
        return remote(down.at[:, p], p_down.at[pl.ds(z * 8, 8)], zd1_s.at[p], zd1_r.at[z], at_z(p))

    def z_up1(p):
        return remote(up.at[:, p], p_up.at[pl.ds(z * 8, 8)], zu1_s.at[p], zu1_r.at[z], at_z(p))

    def z_down2(p):
        return remote(s_down.at[p], a_down.at[:, z], zd2_s.at[p], zd2_r.at[z], at_z(p))

    def z_up2(p):
        return remote(s_up.at[p], a_up.at[:, z], zu2_s.at[p], zu2_r.at[z], at_z(p))

    def each_z(make):
        def body(i, _):
            make(lax.rem(z + i, NZ))
            return 0
        lax.fori_loop(1, NZ, body, 0)

    def got(dst, sem):
        pltpu.make_async_copy(dst, dst, sem).wait()

    for q in range(4):
        swap_h(q).start()
    swap_w(blk(2, 2)).start()
    each_z(lambda p: z_slot(p).start())
    each_z(lambda p: z_down1(p).start())
    for ox, oy in BLOCK_ORDER[1:]:
        swap_w(blk(ox, oy)).start()
    each_z(lambda p: z_up1(p).start())

    def product(q, b):
        r = pl.ds(pl.multiple_of(q * 256, 256), 256)
        return jnp.dot(h_own[r, :], w_own[b], preferred_element_type=F32) + jnp.dot(
            h_sib[r, :], w_sib[b], preferred_element_type=F32
        )

    def order(j):
        return jnp.where(j == 0, 2, jnp.where(j == 1, 1, jnp.where(j == 2, 3, 0)))

    def block_of(f, along, across):
        first = f // 2 == 0
        return blk(jnp.where(first, along, across), jnp.where(first, across, along))

    def ahead(f):
        return jnp.where(lax.rem(f, 2) == 0, 1, 3)

    def other(f):
        return f + 1 - 2 * lax.rem(f, 2)

    def peer1(f):
        first = f // 2 == 0
        d = ahead(f)
        return at(x + jnp.where(first, d, 0), y + jnp.where(first, 0, d), core)

    def peer2(f):
        first = f // 2 == 0
        d = ahead(f)
        return at(x + jnp.where(first, 0, d), y + jnp.where(first, d, 0), core)

    def copy1(f, s, j):
        return remote(send1.at[f, s, j], recv1.at[f, s, j], s1_s.at[f, s, j], s1_r.at[f, s, j], peer1(f))

    def copy2(f, s):
        return remote(send2.at[f, s], recv2.at[f, s], s2_s.at[f, s], s2_r.at[f, s], peer2(f))

    for q in range(4):
        load_h(q).wait()
        swap_h(q).wait_recv()

    def need_w(b):
        load_w(b).wait()
        swap_w(b).wait_recv()

    def step0(i, _):
        j = i // 4
        f = lax.rem(i, 4)
        o = order(j)

        @pl.when(f == 0)
        def _():
            need_w(blk(2, o))

        @pl.when((f == 2) & (j > 0))
        def _():
            need_w(blk(o, 2))

        send1[f, 0, j] = product(f, block_of(f, 2, o)).astype(BF)
        copy1(f, 0, j).start()
        return 0

    lax.fori_loop(0, 16, step0, 0)
    for ox, oy in BLOCK_ORDER[7:]:
        need_w(blk(ox, oy))

    def step1(i, _):
        j = i // 4
        f = lax.rem(i, 4)
        send1[f, 1, j] = product(other(f), block_of(f, ahead(f), order(j))).astype(BF)
        copy1(f, 1, j).start()
        return 0

    lax.fori_loop(0, 16, step1, 0)

    def step2(i, _):
        j = i // 4
        f = lax.rem(i, 4)
        v = product(f, block_of(f, ahead(f), order(j)))
        copy1(f, 0, j).wait_recv()
        send1[f, 2, j] = (v + recv1[f, 0, j].astype(F32)).astype(BF)
        copy1(f, 2, j).start()
        return 0

    lax.fori_loop(0, 16, step2, 0)

    def take_slots(p):
        got(slot_in.at[p], zs_r.at[p])
        cp = pltpu.make_async_copy(slot_in.at[p], slot_s.at[p], loc_sem.at[2])
        cp.start()
        cp.wait()

    each_z(take_slots)
    cp = pltpu.make_async_copy(slot_out, slot_s.at[z], loc_sem.at[2])
    cp.start()
    cp.wait()

    own_down.wait()
    each_z(lambda p: got(p_down.at[pl.ds(p * 8, 8)], zd1_r.at[p]))

    def choose(src, dst):
        def body_for(p):
            def body(i, _):
                dst[p, i] = src[slot_s[p, i, 0]]
                return 0
            lax.fori_loop(0, 8, body, 0)
        return body_for

    def send_down(p):
        choose(p_down, s_down)(p)
        z_down2(p).start()

    each_z(send_down)

    def keep_down(i, _):
        a_down[i, z] = p_down[slot_s[z, i, 0]]
        a_up[i, z] = p_up[slot_s[z, i, 0]]
        return 0

    def step3(i, _):
        j = i // 4
        f = lax.rem(i, 4)
        part[f, j] = product(f, block_of(f, 0, order(j)))
        return 0

    lax.fori_loop(0, 16, step3, 0)

    own_up.wait()
    each_z(lambda p: got(p_up.at[pl.ds(p * 8, 8)], zu1_r.at[p]))

    def send_up(p):
        choose(p_up, s_up)(p)
        z_up2(p).start()

    each_z(send_up)
    lax.fori_loop(0, 8, keep_down, 0)

    def total1(q, j):
        copy1(q, 2, j).wait_recv()
        copy1(other(q), 1, j).wait_recv()
        return part[q, j] + recv1[q, 2, j].astype(F32) + recv1[other(q), 1, j].astype(F32)

    def turn0(q, _):
        send2[q, 0] = total1(q, 0).astype(BF)
        copy2(q, 0).start()
        return 0

    lax.fori_loop(0, 4, turn0, 0)

    def turn1(i, _):
        j = 1 + i // 4
        q = lax.rem(i, 4)
        v = total1(q, j)
        keep = lax.rem(q, 2) == j - 1

        @pl.when(keep)
        def _():
            hold[q] = v

        @pl.when(jnp.logical_not(keep))
        def _():
            send2[other(q), 1] = v.astype(BF)
            copy2(other(q), 1).start()

        return 0

    lax.fori_loop(0, 8, turn1, 0)

    def turn2(q, _):
        v = hold[q]
        copy2(q, 0).wait_recv()
        send2[q, 2] = (v + recv2[q, 0].astype(F32)).astype(BF)
        copy2(q, 2).start()
        return 0

    lax.fori_loop(0, 4, turn2, 0)

    def turn3(q, _):
        part[q, 3] = total1(q, 3)
        return 0

    lax.fori_loop(0, 4, turn3, 0)

    each_z(lambda p: got(a_down.at[:, p], zd2_r.at[p]))

    def rank(i, _):
        r = pl.ds(pl.multiple_of(i * 128, 128), 128)
        v = lax.dot_general(
            a_down[i].reshape(64, 640), h_own[r, :], (((1,), (1,)), ((), ())),
            preferred_element_type=F32,
        )
        rank_out[pl.ds(i * 4, 4)] = v.astype(BF).reshape(4, 16, 128)
        return 0

    lax.fori_loop(0, 8, rank, 0)

    def copy_a(p):
        return remote(rank_out.at[p], rank_in.at[t], ra_s.at[p], ra_r.at[t], at_t(p))

    def copy_b(p):
        return remote(rank_sum, rank_all.at[t], rb_s.at[p], rb_r.at[t], at_t(p))

    def each_t(make):
        def body(i, _):
            make(lax.rem(t + i, NTP))
            return 0
        lax.fori_loop(1, NTP, body, 0)

    each_t(lambda p: copy_a(p).start())
    each_t(lambda p: got(rank_in.at[p], ra_r.at[p]))

    def add_rank(i, acc):
        return acc + rank_in[lax.rem(t + i, NTP)].astype(F32)

    total = lax.fori_loop(1, NTP, add_rank, rank_out[t].astype(F32)).astype(BF)
    rank_sum[...] = total
    rank_all[t] = total
    each_t(lambda p: copy_b(p).start())
    each_z(lambda p: got(a_up.at[:, p], zu2_r.at[p]))
    each_t(lambda p: got(rank_all.at[p], rb_r.at[p]))

    def finish(q, _):
        copy2(q, 2).wait_recv()
        copy2(other(q), 1).wait_recv()
        base = part[q, 3] + recv2[q, 2].astype(F32) + recv2[other(q), 1].astype(F32)
        for k in range(2):
            i = q * 2 + k
            v = lax.dot_general(
                rank_all[pl.ds(i * 4, 4)].reshape(64, 128), a_up[i].reshape(64, 256),
                (((0,), (0,)), ((), ())), preferred_element_type=F32,
            )
            delta = (v * adapter_scale).astype(BF).astype(F32)
            r = pl.ds(pl.multiple_of(i * 128, 128), 128)
            out[r, :] = (base[k * 128:(k + 1) * 128] + delta).astype(BF)
        return 0

    lax.fori_loop(0, 4, finish, 0)

    for q in range(4):
        swap_h(q).wait_send()

    def sent_w(b, _):
        swap_w(b).wait_send()
        return 0

    lax.fori_loop(0, 16, sent_w, 0)

    def sent1(i, _):
        f = i // 12
        s = lax.rem(i // 4, 3)
        copy1(f, s, lax.rem(i, 4)).wait_send()
        return 0

    lax.fori_loop(0, 48, sent1, 0)

    def sent2(i, _):
        copy2(i // 3, lax.rem(i, 3)).wait_send()
        return 0

    lax.fori_loop(0, 12, sent2, 0)

    def sent_z(p):
        z_slot(p).wait_send()
        z_down1(p).wait_send()
        z_up1(p).wait_send()
        z_down2(p).wait_send()
        z_up2(p).wait_send()

    each_z(sent_z)

    def sent_t(p):
        copy_a(p).wait_send()
        copy_b(p).wait_send()

    each_t(sent_t)


def local(hidden, down_weight, adapter_down_factor, adapter_up_factor, row_tile_adapter, adapter_pool_slot):
    any_ = pl.BlockSpec(memory_space=pl.ANY)
    smem = pl.BlockSpec(memory_space=pltpu.SMEM)
    V, D = pltpu.VMEM, pltpu.SemaphoreType.DMA
    down = adapter_down_factor.reshape(8, 8, 8, 640)
    up = adapter_up_factor.reshape(8, 8, 8, 256)
    return pl.pallas_call(
        kernel,
        out_shape=jax.ShapeDtypeStruct((1024, 256), BF),
        in_specs=[any_, any_, any_, any_, smem, smem],
        out_specs=pl.BlockSpec(memory_space=pltpu.VMEM),
        scratch_shapes=[
            V((1024, 640), BF), V((1024, 640), BF),
            V((16, 640, 256), BF), V((16, 640, 256), BF),
            V((4, 3, 4, 256, 256), BF), V((4, 3, 4, 256, 256), BF),
            V((4, 3, 256, 256), BF), V((4, 3, 256, 256), BF),
            V((4, 4, 256, 256), F32), V((4, 256, 256), F32),
            V((64, 8, 640), BF), V((8, 8, 8, 640), BF), V((8, 8, 8, 640), BF),
            V((64, 8, 256), BF), V((8, 8, 8, 256), BF), V((8, 8, 8, 256), BF),
            V((8, 128), jnp.int32), V((8, 8, 128), jnp.int32), pltpu.SMEM((8, 8, 128), jnp.int32),
            V((32, 16, 128), BF), V((32, 16, 128), BF), V((16, 128), BF), V((32, 16, 128), BF),
            D((20,)), D((4,)), D((4,)), D((16,)), D((16,)),
            D((4, 3, 4)), D((4, 3, 4)), D((4, 3)), D((4, 3)),
            D((8,)), D((8,)), D((8,)), D((8,)), D((8,)), D((8,)),
            D((8,)), D((8,)), D((8,)), D((8,)),
            D((32,)), D((32,)), D((32,)), D((32,)), D((3,)),
        ],
        compiler_params=pltpu.CompilerParams(
            collective_id=0, has_side_effects=True, vmem_limit_bytes=60 * 2**20
        ),
    )(hidden, down_weight, down, up, row_tile_adapter, adapter_pool_slot)


def solution(mesh):
    placed = (
        P("grp", "tp"), P("tp", None), P("grp", None, "tp"), P("grp", None, "tp"), P("grp"), P(),
    )
    return jax.shard_map(local, mesh=mesh, in_specs=placed, out_specs=P("grp", "tp"), check_vma=False)
```

time: 367 us -> 80.2 us (0.22)
  waiting for transfers between devices: 320 us -> 0 us
  Pallas kernels: 0 us -> 78.2 us
  matrix products: 22.6 us -> 0 us
  between operations: 13.2 us -> 0.01 us
  local copies, waits for them, and re-layouts: 7.93 us -> 1.87 us
    reduce_scatter x1 -> x0, waiting for transfers between devices: 124 us -> none  [local(): lax.psum_scatter(lax.dot_general(down_weight, hidden, (((0,), (1,)), ((),...]
    psum x1 -> x0, waiting for transfers between devices: 115 us -> none  [local(): rank_projections = lax.psum(rank_part.astype(jnp.bfloat16), 'tp')]
    all_gather x2 -> x0, waiting for transfers between devices: 79.9 us -> none  [the longest x1 67.3 us: local(): lax.all_gather(adapter_down_factor, 'grp', axis=0, tiled=True)]
    pallas_call x0 -> x1, Pallas kernels: none -> 78.2 us  [local(): pl.pallas_call(kernel, out_shape=jax.ShapeDtypeStruct((1024, 256), BF), i...]
    dot_general x3 -> x0, matrix products: 22.6 us -> none  [the longest x1 20.1 us: local(): lax.dot_general(down_weight, hidden, (((0,), (1,)), ((), ())), preferred_...]
    gather x3 -> x0, local copies, waits for them, and re-layouts: 6.6 us -> none  [the longest x1 3.15 us: local(): pooled_down[slot_table]]
  transfers between devices with their start and end apart: 4 -> 0, of which waited for: 4 -> 0; matrix products, arithmetic and copies ran while one was open for 8% -> 0% of each run, Pallas kernels for 0% -> 0%
where the time goes in v1:
time: 80.2 us; the launch traced here: 80 us
  Pallas kernels  78.2 us (98%)
  local copies, waits for them, and re-layouts  1.87 us (2%)
    pallas_call x1, Pallas kernels, local(): pl.pallas_call(kernel, out_shape=jax.ShapeDtypeStruct((1024, 256), BF), i...  78.2 us
    unnamed x1, local copies, waits for them, and re-layouts  1.87 us

profile of v1, /device:TPU:1, one launch (start us, length us, event | category | flops | bytes accessed | tf_op | source)
XLA Modules:
  0.0 80.0 jit_solution(15547417057980748980)
XLA Ops:
  0.0 78.2 %shard_map.64 = bf16[1024,256]{1,0:T(8,128)(2,1)} custom-call(bf16[1024,640]{1,0:T(8,128)(2,1)} %hid.1, bf16[640,8192]{1,0:T(8,128)(2,1)} %wgt.1, bf16[8,8,8,640]{3,2,1,0:T(8,128)(2,1)} %bitcast.2, bf16[8,8,8,256]{3,2,1,0:T(8,128)(2,1)} %bitcast.3, s32[8]{0:T(128)} %tiles.1, s32[64]{0:T(128)} %slots.1), custom_call_target="tpu_custom_call" | custom-call | tf_op jit(solution)/shard_map/pallas_call | solution.py:412
  78.2 1.9 %copy.8 = bf16[1024,256]{1,0:T(8,128)(2,1)} copy(bf16[1024,256]{1,0:T(8,128)(2,1)} %shard_map.64) | data formatting | bytes 1048576

commit v2 on v1

--- a/solution.py
+++ b/solution.py
@@ -9,6 +9,7 @@
 MESH = pl.DeviceIdType.MESH
 NX, NY, NZ, NTP = 4, 4, 8, 32
 BF, F32 = jnp.bfloat16, jnp.float32
+DEPTH = 4
 BLOCK_ORDER = (
     (2, 2), (2, 1), (1, 2), (2, 3), (3, 2), (2, 0), (0, 2), (1, 1),
     (1, 3), (3, 1), (3, 3), (1, 0), (3, 0), (0, 1), (0, 3), (0, 0),
@@ -22,7 +23,7 @@
     rank_out, rank_in, rank_sum, rank_all,
     l_sem, hs_s, hs_r, ws_s, ws_r, s1_s, s1_r, s2_s, s2_r,
     zs_s, zs_r, zd1_s, zd1_r, zu1_s, zu1_r, zd2_s, zd2_r, zu2_s, zu2_r,
-    ra_s, ra_r, rb_s, rb_r, loc_sem,
+    ra_s, ra_r, rb_s, rb_r, loc_sem, slot_sem, ready_p, ready_z,
 ):
     z = lax.axis_index("grp")
     t = lax.axis_index("tp")
@@ -83,17 +84,24 @@
 
     barrier = pltpu.get_barrier_semaphore()
 
-    def greet_t(i, _):
-        pl.semaphore_signal(barrier, inc=1, device_id=at_t(lax.rem(t + i, NTP)), device_id_type=MESH)
-        return 0
-
-    def greet_z(i, _):
-        pl.semaphore_signal(barrier, inc=1, device_id=at_z(lax.rem(z + i, NZ)), device_id_type=MESH)
-        return 0
-
-    lax.fori_loop(1, NZ, greet_z, 0)
-    lax.fori_loop(1, NTP, greet_t, 0)
-    pl.semaphore_wait(barrier, NTP - 1 + NZ - 1)
+    near_plane = [sib] + [at(x + d, y, core) for d in (1, 3)] + [at(x, y + d, core) for d in (1, 3)]
+    near_z = [at_z(lax.rem(z + d, NZ)) for d in (1, NZ - 1)]
+
+    def tell(sem, devices):
+        for dev in devices:
+            pl.semaphore_signal(sem, inc=1, device_id=dev, device_id_type=MESH)
+
+    tell(barrier, near_plane + near_z)
+    pl.semaphore_wait(barrier, 7)
+
+    def hear_plane(k):
+        pl.semaphore_wait(ready_p.at[k], 5)
+
+    def hear_z(k):
+        pl.semaphore_wait(ready_z.at[k], 2)
+
+    tell(ready_z.at[0], near_z)
+    tell(ready_p.at[0], near_plane)
 
     def z_slot(p):
         return remote(slot_out, slot_in.at[z], zs_s.at[p], zs_r.at[z], at_z(p))
@@ -119,14 +127,35 @@
     def got(dst, sem):
         pltpu.make_async_copy(dst, dst, sem).wait()
 
+    def start1(d):
+        for dd in (d, NZ - d) if d < NZ // 2 else (d,):
+            p = lax.rem(z + dd, NZ)
+            z_slot(p).start()
+            z_down1(p).start()
+
+    def ring_z(d):
+        return [lax.rem(z + dd, NZ) for dd in ((d, NZ - d) if d < NZ // 2 else (d,))]
+
+    def start1(d):
+        for p in ring_z(d):
+            z_slot(p).start()
+            z_down1(p).start()
+
+    def start_up(d):
+        for p in ring_z(d):
+            z_up1(p).start()
+
     for q in range(4):
         swap_h(q).start()
     swap_w(blk(2, 2)).start()
-    each_z(lambda p: z_slot(p).start())
-    each_z(lambda p: z_down1(p).start())
-    for ox, oy in BLOCK_ORDER[1:]:
+    start1(1)
+    for ox, oy in BLOCK_ORDER[1:7]:
         swap_w(blk(ox, oy)).start()
-    each_z(lambda p: z_up1(p).start())
+    hear_z(0)
+    tell(ready_z.at[1], near_z)
+    start1(2)
+    for ox, oy in BLOCK_ORDER[7:]:
+        swap_w(blk(ox, oy)).start()
 
     def product(q, b):
         r = pl.ds(pl.multiple_of(q * 256, 256), 256)
@@ -171,6 +200,19 @@
         load_w(b).wait()
         swap_w(b).wait_recv()
 
+    def place(n):
+        late = n - 4
+        return (
+            jnp.where(n < 4, 0, 1 + lax.rem(late, 2)),
+            jnp.where(n < 4, n, late // 2),
+        )
+
+    def hold_back(f, n):
+        @pl.when(n >= DEPTH)
+        def _():
+            s_, j_ = place(n - DEPTH)
+            copy1(f, s_, j_).wait_send()
+
     def step0(i, _):
         j = i // 4
         f = lax.rem(i, 4)
@@ -185,44 +227,64 @@
             need_w(blk(o, 2))
 
         send1[f, 0, j] = product(f, block_of(f, 2, o)).astype(BF)
+        hold_back(f, j)
         copy1(f, 0, j).start()
         return 0
 
-    lax.fori_loop(0, 16, step0, 0)
+    lax.fori_loop(0, 4, step0, 0)
+    hear_z(1)
+    tell(ready_z.at[2], near_z)
+    start1(3)
+    lax.fori_loop(4, 8, step0, 0)
+    hear_z(2)
+    start1(4)
+    start_up(1)
+    start_up(2)
+    lax.fori_loop(8, 16, step0, 0)
+    hear_plane(0)
+    tell(ready_p.at[1], near_plane)
     for ox, oy in BLOCK_ORDER[7:]:
         need_w(blk(ox, oy))
 
-    def step1(i, _):
-        j = i // 4
-        f = lax.rem(i, 4)
-        send1[f, 1, j] = product(other(f), block_of(f, ahead(f), order(j))).astype(BF)
-        copy1(f, 1, j).start()
-        return 0
-
-    lax.fori_loop(0, 16, step1, 0)
-
-    def step2(i, _):
-        j = i // 4
-        f = lax.rem(i, 4)
-        v = product(f, block_of(f, ahead(f), order(j)))
-        copy1(f, 0, j).wait_recv()
-        send1[f, 2, j] = (v + recv1[f, 0, j].astype(F32)).astype(BF)
-        copy1(f, 2, j).start()
-        return 0
-
-    lax.fori_loop(0, 16, step2, 0)
+    def both(j):
+        def step1(f, _):
+            send1[f, 1, j] = product(other(f), block_of(f, ahead(f), order(j))).astype(BF)
+            hold_back(f, 4 + 2 * j)
+            copy1(f, 1, j).start()
+            return 0
+
+        def step2(f, _):
+            v = product(f, block_of(f, ahead(f), order(j)))
+            copy1(f, 0, j).wait_recv()
+            send1[f, 2, j] = (v + recv1[f, 0, j].astype(F32)).astype(BF)
+            hold_back(f, 5 + 2 * j)
+            copy1(f, 2, j).start()
+            return 0
+
+        lax.fori_loop(0, 4, step1, 0)
+        lax.fori_loop(0, 4, step2, 0)
+
+    def both_loop(j, _):
+        both(j)
+        return 0
+
+    lax.fori_loop(0, 2, both_loop, 0)
+    hear_plane(1)
+    tell(ready_p.at[2], near_plane)
+
+    def slot_copy(p):
+        return pltpu.make_async_copy(slot_in.at[p], slot_s.at[p], slot_sem.at[p])
+
+    own_slots = pltpu.make_async_copy(slot_out, slot_s.at[z], loc_sem.at[2])
+    own_slots.start()
 
     def take_slots(p):
         got(slot_in.at[p], zs_r.at[p])
-        cp = pltpu.make_async_copy(slot_in.at[p], slot_s.at[p], loc_sem.at[2])
-        cp.start()
-        cp.wait()
+        slot_copy(p).start()
 
     each_z(take_slots)
-    cp = pltpu.make_async_copy(slot_out, slot_s.at[z], loc_sem.at[2])
-    cp.start()
-    cp.wait()
-
+    each_z(lambda p: slot_copy(p).wait())
+    own_slots.wait()
     own_down.wait()
     each_z(lambda p: got(p_down.at[pl.ds(p * 8, 8)], zd1_r.at[p]))
 
@@ -239,11 +301,18 @@
         z_down2(p).start()
 
     each_z(send_down)
+    start_up(3)
+    start_up(4)
 
     def keep_down(i, _):
         a_down[i, z] = p_down[slot_s[z, i, 0]]
+        return 0
+
+    def keep_up(i, _):
         a_up[i, z] = p_up[slot_s[z, i, 0]]
         return 0
+
+    lax.fori_loop(0, 8, keep_down, 0)
 
     def step3(i, _):
         j = i // 4
@@ -251,17 +320,10 @@
         part[f, j] = product(f, block_of(f, 0, order(j)))
         return 0
 
-    lax.fori_loop(0, 16, step3, 0)
-
-    own_up.wait()
-    each_z(lambda p: got(p_up.at[pl.ds(p * 8, 8)], zu1_r.at[p]))
-
-    def send_up(p):
-        choose(p_up, s_up)(p)
-        z_up2(p).start()
-
-    each_z(send_up)
-    lax.fori_loop(0, 8, keep_down, 0)
+    lax.fori_loop(2, 3, both_loop, 0)
+    hear_plane(2)
+    tell(ready_p.at[3], near_plane)
+    lax.fori_loop(0, 4, step3, 0)
 
     def total1(q, j):
         copy1(q, 2, j).wait_recv()
@@ -274,6 +336,10 @@
         return 0
 
     lax.fori_loop(0, 4, turn0, 0)
+
+    lax.fori_loop(3, 4, both_loop, 0)
+    hear_plane(3)
+    lax.fori_loop(4, 16, step3, 0)
 
     def turn1(i, _):
         j = 1 + i // 4
@@ -302,12 +368,6 @@
         return 0
 
     lax.fori_loop(0, 4, turn2, 0)
-
-    def turn3(q, _):
-        part[q, 3] = total1(q, 3)
-        return 0
-
-    lax.fori_loop(0, 4, turn3, 0)
 
     each_z(lambda p: got(a_down.at[:, p], zd2_r.at[p]))
 
@@ -335,6 +395,38 @@
         lax.fori_loop(1, NTP, body, 0)
 
     each_t(lambda p: copy_a(p).start())
+
+    def turn3(q, _):
+        part[q, 3] = total1(q, 3)
+        return 0
+
+    for q in range(4):
+        swap_h(q).wait_send()
+
+    def sent_w(b, _):
+        swap_w(b).wait_send()
+        return 0
+
+    lax.fori_loop(0, 16, sent_w, 0)
+
+    def sent_z(p):
+        z_slot(p).wait_send()
+        z_down1(p).wait_send()
+        z_up1(p).wait_send()
+        z_down2(p).wait_send()
+
+    each_z(sent_z)
+    own_up.wait()
+    each_z(lambda p: got(p_up.at[pl.ds(p * 8, 8)], zu1_r.at[p]))
+
+    def send_up(p):
+        choose(p_up, s_up)(p)
+        z_up2(p).start()
+
+    each_z(send_up)
+    lax.fori_loop(0, 8, keep_up, 0)
+
+    lax.fori_loop(0, 4, turn3, 0)
     each_t(lambda p: got(rank_in.at[p], ra_r.at[p]))
 
     def add_rank(i, acc):
@@ -364,22 +456,12 @@
 
     lax.fori_loop(0, 4, finish, 0)
 
-    for q in range(4):
-        swap_h(q).wait_send()
-
-    def sent_w(b, _):
-        swap_w(b).wait_send()
-        return 0
-
-    lax.fori_loop(0, 16, sent_w, 0)
-
     def sent1(i, _):
-        f = i // 12
-        s = lax.rem(i // 4, 3)
-        copy1(f, s, lax.rem(i, 4)).wait_send()
-        return 0
-
-    lax.fori_loop(0, 48, sent1, 0)
+        s_, j_ = place(12 - DEPTH + i // 4)
+        copy1(lax.rem(i, 4), s_, j_).wait_send()
+        return 0
+
+    lax.fori_loop(0, 4 * DEPTH, sent1, 0)
 
     def sent2(i, _):
         copy2(i // 3, lax.rem(i, 3)).wait_send()
@@ -387,14 +469,7 @@
 
     lax.fori_loop(0, 12, sent2, 0)
 
-    def sent_z(p):
-        z_slot(p).wait_send()
-        z_down1(p).wait_send()
-        z_up1(p).wait_send()
-        z_down2(p).wait_send()
-        z_up2(p).wait_send()
-
-    each_z(sent_z)
+    each_z(lambda p: z_up2(p).wait_send())
 
     def sent_t(p):
         copy_a(p).wait_send()
@@ -428,7 +503,8 @@
             D((4, 3, 4)), D((4, 3, 4)), D((4, 3)), D((4, 3)),
             D((8,)), D((8,)), D((8,)), D((8,)), D((8,)), D((8,)),
             D((8,)), D((8,)), D((8,)), D((8,)),
-            D((32,)), D((32,)), D((32,)), D((32,)), D((3,)),
+            D((32,)), D((32,)), D((32,)), D((32,)), D((3,)), D((8,)),
+            pltpu.SemaphoreType.REGULAR((4,)), pltpu.SemaphoreType.REGULAR((3,)),
         ],
         compiler_params=pltpu.CompilerParams(
             collective_id=0, has_side_effects=True, vmem_limit_bytes=60 * 2**20

time: 80.2 us -> 75.3 us (0.939)
  Pallas kernels: 78.2 us -> 73.3 us
    pallas_call x1, Pallas kernels: 78.2 us -> 73.3 us  [local(): pl.pallas_call(kernel, out_shape=jax.ShapeDtypeStruct((1024, 256), BF), i...]
where the time goes in v2:
time: 75.3 us; the launch traced here: 75.2 us
  Pallas kernels  73.3 us (97%)
  local copies, waits for them, and re-layouts  1.87 us (2%)
    pallas_call x1, Pallas kernels, local(): pl.pallas_call(kernel, out_shape=jax.ShapeDtypeStruct((1024, 256), BF), i...  73.3 us
    unnamed x1, local copies, waits for them, and re-layouts  1.87 us

profile of v2, /device:TPU:1, one launch (start us, length us, event | category | flops | bytes accessed | tf_op | source)
XLA Modules:
  0.0 75.2 jit_solution(10391152674631171773)
XLA Ops:
  0.0 73.3 %shard_map.64 = bf16[1024,256]{1,0:T(8,128)(2,1)} custom-call(bf16[1024,640]{1,0:T(8,128)(2,1)} %hid.1, bf16[640,8192]{1,0:T(8,128)(2,1)} %wgt.1, bf16[8,8,8,640]{3,2,1,0:T(8,128)(2,1)} %bitcast.2, bf16[8,8,8,256]{3,2,1,0:T(8,128)(2,1)} %bitcast.3, s32[8]{0:T(128)} %tiles.1, s32[64]{0:T(128)} %slots.1), custom_call_target="tpu_custom_call" | custom-call | tf_op jit(solution)/shard_map/pallas_call | solution.py:487
  73.3 1.9 %copy.8 = bf16[1024,256]{1,0:T(8,128)(2,1)} copy(bf16[1024,256]{1,0:T(8,128)(2,1)} %shard_map.64) | data formatting | bytes 1048576

commit v3 on v2

v3 whole, which is shorter than its diff:
```python
import jax
import jax.numpy as jnp
from jax import lax
from jax.experimental import pallas as pl
from jax.experimental.pallas import tpu as pltpu
from jax.sharding import PartitionSpec as P

adapter_scale = 2.0
MESH = pl.DeviceIdType.MESH
NX, NY, NZ, NTP = 4, 4, 8, 32
BF, F32 = jnp.bfloat16, jnp.float32
DEPTH = 4
CUT = 384
GROUPS = (
    ((2, 2),), ((2, 1), (1, 2)), ((2, 3), (3, 2)), ((2, 0), (0, 2)),
    ((1, 1), (1, 3), (3, 1), (3, 3), (1, 0), (3, 0), (0, 1), (0, 3), (0, 0)),
)


def kernel(
    hid, wgt, down, up, tiles, slots, out,
    h_own, h_sib, w_own, w_sib, send1, recv1, send2, recv2, part, hold,
    p_da, s_da, a_da, p_db, s_db, a_db, p_up, s_up, a_up, slot_out, slot_in, slot_s,
    rank_out, rank_in, rank_sum, rank_all,
    h_l, h_s, h_r, w_l, w_s, w_r, s1_s, s1_r, s2_s, s2_r, z_s, z_r, r_s, r_r, loc_sem,
    ready_p, ready_z,
):
    z = lax.axis_index("grp")
    t = lax.axis_index("tp")
    core = lax.rem(t, 2)
    y = lax.rem(t // 2, NY)
    x = t // (2 * NY)

    def at(xx, yy, cc):
        return {"grp": z, "tp": (lax.rem(xx, NX) * NY + lax.rem(yy, NY)) * 2 + cc}

    def at_z(zz):
        return {"grp": zz, "tp": t}

    def at_t(tt):
        return {"grp": z, "tp": tt}

    def remote(src, dst, ssem, rsem, dev):
        return pltpu.make_async_remote_copy(
            src_ref=src, dst_ref=dst, send_sem=ssem, recv_sem=rsem,
            device_id=dev, device_id_type=MESH,
        )

    def got(ref, sem):
        pltpu.make_async_copy(ref, ref, sem).wait()

    sib = at(x, y, 1 - core)

    def blk(ox, oy):
        return lax.rem(x + ox, NX) * NY + lax.rem(y + oy, NY)

    def load_h(q):
        r = pl.ds(q * 256, 256)
        return pltpu.make_async_copy(hid.at[r], h_own.at[r], h_l.at[q])

    def load_w(b, g):
        c = pl.multiple_of((2 * b + core) * 256, 256)
        return pltpu.make_async_copy(wgt.at[:, pl.ds(c, 256)], w_own.at[b], w_l.at[g])

    def swap_h(q):
        r = pl.ds(q * 256, 256)
        return remote(hid.at[r], h_sib.at[r], h_s, h_r.at[q], sib)

    def swap_w(b, g):
        c = pl.multiple_of((2 * b + 1 - core) * 256, 256)
        return remote(wgt.at[:, pl.ds(c, 256)], w_sib.at[b], w_s, w_r.at[g], sib)

    for q in range(4):
        load_h(q).start()
    for g, group in enumerate(GROUPS):
        for ox, oy in group:
            load_w(blk(ox, oy), g).start()

    row = lax.broadcasted_iota(jnp.int32, (8, 128), 0)
    mine = jnp.zeros((8, 128), jnp.int32)
    for i in range(8):
        mine = jnp.where(row == i, slots[tiles[i]], mine)
    slot_out[...] = mine

    barrier = pltpu.get_barrier_semaphore()
    near_plane = [sib] + [at(x + d, y, core) for d in (1, 3)] + [at(x, y + d, core) for d in (1, 3)]
    near_z = [at_z(lax.rem(z + d, NZ)) for d in (1, NZ - 1)]

    def tell(sem, devices):
        for dev in devices:
            pl.semaphore_signal(sem, inc=1, device_id=dev, device_id_type=MESH)

    tell(barrier, near_plane + near_z)
    pl.semaphore_wait(barrier, 7)

    def hear_plane(k):
        pl.semaphore_wait(ready_p.at[k], 5)

    def hear_z(k):
        pl.semaphore_wait(ready_z.at[k], 2)

    LA, LB = pl.ds(0, CUT), pl.ds(CUT, 640 - CUT)

    def ends(n, p):
        mine_at = pl.ds(z * 8, 8)
        return (
            (slot_out, slot_in.at[z]),
            (down.at[:, p, :, LA], p_da.at[mine_at]),
            (down.at[:, p, :, LB], p_db.at[mine_at]),
            (up.at[:, p], p_up.at[mine_at]),
            (s_da.at[p], a_da.at[:, z]),
            (s_db.at[p], a_db.at[:, z]),
            (s_up.at[p], a_up.at[:, z]),
        )[n]

    whole = (slot_in, p_da, p_db, p_up, a_da, a_db, a_up)
    others = (
        slot_in.at[pl.ds(0, 7)], p_da.at[pl.ds(0, 56)], p_db.at[pl.ds(0, 56)], p_up.at[pl.ds(0, 56)],
        s_da.at[pl.ds(0, 7)], s_db.at[pl.ds(0, 7)], s_up.at[pl.ds(0, 7)],
    )

    def z_send(n, p):
        src, dst = ends(n, p)
        remote(src, dst, z_s.at[n], z_r.at[n], at_z(p)).start()

    def z_keep(n):
        src, dst = ends(n, z)
        pltpu.make_async_copy(src, dst, z_r.at[n]).start()

    def z_got(n):
        got(whole[n], z_r.at[n])

    def z_sent(n):
        got(others[n], z_s.at[n])

    def ring_z(d):
        return [lax.rem(z + dd, NZ) for dd in ((d, NZ - d) if d < NZ // 2 else (d,))]

    def start1(d):
        for n in (0, 1, 2):
            for p in ring_z(d):
                z_send(n, p)

    tell(ready_z.at[0], near_z)
    swap_h(0).start()
    swap_w(blk(2, 2), 0).start()
    for q in range(1, 4):
        swap_h(q).start()
    start1(1)
    for g in (1, 2, 3):
        for ox, oy in GROUPS[g]:
            swap_w(blk(ox, oy), g).start()
    tell(ready_p.at[0], near_plane)
    for n in (0, 1, 2, 3):
        z_keep(n)
    hear_z(0)
    tell(ready_z.at[1], near_z)
    start1(2)
    for ox, oy in GROUPS[4]:
        swap_w(blk(ox, oy), 4).start()

    def product(q, b):
        r = pl.ds(pl.multiple_of(q * 256, 256), 256)
        return jnp.dot(h_own[r, :], w_own[b], preferred_element_type=F32) + jnp.dot(
            h_sib[r, :], w_sib[b], preferred_element_type=F32
        )

    def order(j):
        return jnp.where(j == 0, 2, jnp.where(j == 1, 1, jnp.where(j == 2, 3, 0)))

    def block_of(f, along, across):
        first = f // 2 == 0
        return blk(jnp.where(first, along, across), jnp.where(first, across, along))

    def ahead(f):
        return jnp.where(lax.rem(f, 2) == 0, 1, 3)

    def other(f):
        return f + 1 - 2 * lax.rem(f, 2)

    def peer1(f):
        first = f // 2 == 0
        d = ahead(f)
        return at(x + jnp.where(first, d, 0), y + jnp.where(first, 0, d), core)

    def peer2(f):
        first = f // 2 == 0
        d = ahead(f)
        return at(x + jnp.where(first, 0, d), y + jnp.where(first, d, 0), core)

    def send_1(f, s, j, n):
        @pl.when(n >= DEPTH)
        def _():
            got(send1.at[0, 0, 0], s1_s.at[f, lax.rem(n, DEPTH)])

        rsem = s1_r.at[0, f, j] if s == 0 else s1_r.at[1, other(f) if s == 1 else f, j]
        remote(
            send1.at[f, s, j], recv1.at[f, s, j], s1_s.at[f, lax.rem(n, DEPTH)], rsem, peer1(f)
        ).start()

    def send_2(f, s):
        rsem = s2_r.at[0, f] if s == 0 else s2_r.at[1, other(f) if s == 1 else f]
        remote(send2.at[f, s], recv2.at[f, s], s2_s, rsem, peer2(f)).start()

    def need_w(g, n):
        got(w_own.at[pl.ds(0, n)], w_l.at[g])
        got(w_sib.at[pl.ds(0, n)], w_r.at[g])

    def step0(i, _):
        j = i // 4
        f = lax.rem(i, 4)

        @pl.when(j == 0)
        def _():
            got(h_own.at[pl.ds(0, 256)], h_l.at[f])
            got(h_sib.at[pl.ds(0, 256)], h_r.at[f])

        @pl.when(i == 0)
        def _():
            need_w(0, 1)

        @pl.when((f == 0) & (j > 0))
        def _():
            need_w(j, 2)

        send1[f, 0, j] = product(f, block_of(f, 2, order(j))).astype(BF)
        send_1(f, 0, j, j)
        return 0

    lax.fori_loop(0, 4, step0, 0)
    hear_z(1)
    tell(ready_z.at[2], near_z)
    start1(3)
    lax.fori_loop(4, 8, step0, 0)
    hear_z(2)
    start1(4)
    lax.fori_loop(8, 16, step0, 0)
    hear_plane(0)
    tell(ready_p.at[1], near_plane)
    need_w(4, 9)

    def both(j, _):
        def step1(f, _):
            send1[f, 1, j] = product(other(f), block_of(f, ahead(f), order(j))).astype(BF)
            send_1(f, 1, j, 4 + 2 * j)
            return 0

        def step2(f, _):
            v = product(f, block_of(f, ahead(f), order(j)))
            got(recv1.at[f, 0, j], s1_r.at[0, f, j])
            send1[f, 2, j] = (v + recv1[f, 0, j].astype(F32)).astype(BF)
            send_1(f, 2, j, 5 + 2 * j)
            return 0

        lax.fori_loop(0, 4, step1, 0)
        lax.fori_loop(0, 4, step2, 0)
        return 0

    def step3(i, _):
        j = i // 4
        f = lax.rem(i, 4)
        part[f, j] = product(f, block_of(f, 0, order(j)))
        return 0

    def total1(q, j):
        got(recv1.at[q, pl.ds(1, 2), j], s1_r.at[1, q, j])
        return part[q, j] + recv1[q, 2, j].astype(F32) + recv1[other(q), 1, j].astype(F32)

    def turn0(q, _):
        send2[q, 0] = total1(q, 0).astype(BF)
        send_2(q, 0)
        return 0

    def turn1(i, _):
        j = 1 + i // 4
        q = lax.rem(i, 4)
        v = total1(q, j)
        keep = lax.rem(q, 2) == j - 1

        @pl.when(keep)
        def _():
            hold[q] = v

        @pl.when(jnp.logical_not(keep))
        def _():
            send2[other(q), 1] = v.astype(BF)
            send_2(other(q), 1)

        return 0

    def turn2(q, _):
        v = hold[q]
        got(recv2.at[q, 0], s2_r.at[0, q])
        send2[q, 2] = (v + recv2[q, 0].astype(F32)).astype(BF)
        send_2(q, 2)
        return 0

    def turn3(q, _):
        part[q, 3] = total1(q, 3)
        return 0

    def pick(n, src, dst):
        def one(p):
            def body(i, _):
                dst[p, i] = src[slot_s[p, i, 0]]
                return 0
            lax.fori_loop(0, 8, body, 0)

        def send(i, _):
            p = lax.rem(z + i, NZ)
            one(p)
            z_send(n, p)
            return 0

        lax.fori_loop(1, NZ, send, 0)
        one(z)
        z_keep(n)

    lax.fori_loop(0, 1, both, 0)
    z_got(0)
    cp = pltpu.make_async_copy(slot_in, slot_s, loc_sem)
    cp.start()
    hear_plane(1)
    tell(ready_p.at[2], near_plane)
    cp.wait()
    z_got(1)
    pick(4, p_da, s_da)
    lax.fori_loop(1, 2, both, 0)
    z_got(2)
    pick(5, p_db, s_db)

    def start_up(i, _):
        z_send(3, lax.rem(z + i, NZ))
        return 0

    lax.fori_loop(1, NZ, start_up, 0)
    lax.fori_loop(2, 3, both, 0)
    hear_plane(2)
    tell(ready_p.at[3], near_plane)
    lax.fori_loop(0, 4, step3, 0)
    lax.fori_loop(0, 4, turn0, 0)
    lax.fori_loop(3, 4, both, 0)
    hear_plane(3)
    lax.fori_loop(4, 8, step3, 0)
    lax.fori_loop(0, 4, turn1, 0)
    lax.fori_loop(8, 16, step3, 0)

    z_got(4)
    z_got(5)
    nt = (((1,), (1,)), ((), ()))
    for i in range(8):
        r = pl.ds(i * 128, 128)
        v = lax.dot_general(
            a_da[i].reshape(64, CUT), h_own[r, 0:CUT], nt, preferred_element_type=F32
        ) + lax.dot_general(
            a_db[i].reshape(64, 640 - CUT), h_own[r, CUT:640], nt, preferred_element_type=F32
        )
        rank_out[pl.ds(i * 4, 4)] = v.astype(BF).reshape(4, 16, 128)

    def send_a(i, _):
        p = lax.rem(t + i, NTP)
        remote(rank_out.at[p], rank_in.at[t], r_s.at[0], r_r.at[0], at_t(p)).start()
        return 0

    def send_b(i, _):
        p = lax.rem(t + i, NTP)
        remote(rank_sum, rank_all.at[t], r_s.at[1], r_r.at[1], at_t(p)).start()
        return 0

    lax.fori_loop(1, NTP, send_a, 0)
    pltpu.make_async_copy(rank_out.at[t], rank_in.at[t], r_r.at[0]).start()
    lax.fori_loop(4, 8, turn1, 0)
    lax.fori_loop(0, 4, turn2, 0)

    got(h_sib, h_s)
    got(w_sib, w_s)
    for n in range(6):
        z_sent(n)
    z_got(3)
    pick(6, p_up, s_up)
    lax.fori_loop(0, 4, turn3, 0)
    got(rank_in, r_r.at[0])

    def add_rank(i, acc):
        return acc + rank_in[i].astype(F32)

    rank_sum[...] = lax.fori_loop(0, NTP, add_rank, jnp.zeros((16, 128), F32)).astype(BF)
    lax.fori_loop(1, NTP, send_b, 0)
    pltpu.make_async_copy(rank_sum, rank_all.at[t], r_r.at[1]).start()

    def last_base(q, _):
        got(recv2.at[q, pl.ds(1, 2)], s2_r.at[1, q])
        part[q, 3] = part[q, 3] + recv2[q, 2].astype(F32) + recv2[other(q), 1].astype(F32)
        return 0

    lax.fori_loop(0, 4, last_base, 0)

    def sent1(i, _):
        got(send1.at[0, 0, 0], s1_s.at[lax.rem(i, 4), i // 4])
        return 0

    lax.fori_loop(0, 4 * DEPTH, sent1, 0)
    got(send2, s2_s)
    got(rank_in.at[pl.ds(0, NTP - 1)], r_s.at[0])
    z_sent(6)
    z_got(6)
    got(rank_all, r_r.at[1])

    def finish(q, _):
        for k in range(2):
            i = q * 2 + k
            v = lax.dot_general(
                rank_all[pl.ds(i * 4, 4)].reshape(64, 128), a_up[i].reshape(64, 256),
                (((0,), (0,)), ((), ())), preferred_element_type=F32,
            )
            delta = (v * adapter_scale).astype(BF).astype(F32)
            r = pl.ds(pl.multiple_of(i * 128, 128), 128)
            out[r, :] = (part[q, 3, k * 128:(k + 1) * 128] + delta).astype(BF)
        return 0

    lax.fori_loop(0, 4, finish, 0)
    got(rank_in.at[pl.ds(0, NTP - 1)], r_s.at[1])


def local(hidden, down_weight, adapter_down_factor, adapter_up_factor, row_tile_adapter, adapter_pool_slot):
    any_ = pl.BlockSpec(memory_space=pl.ANY)
    smem = pl.BlockSpec(memory_space=pltpu.SMEM)
    V, D = pltpu.VMEM, pltpu.SemaphoreType.DMA
    down = adapter_down_factor.reshape(8, 8, 8, 640)
    up = adapter_up_factor.reshape(8, 8, 8, 256)
    return pl.pallas_call(
        kernel,
        out_shape=jax.ShapeDtypeStruct((1024, 256), BF),
        in_specs=[any_, any_, any_, any_, smem, smem],
        out_specs=pl.BlockSpec(memory_space=pltpu.VMEM),
        scratch_shapes=[
            V((1024, 640), BF), V((1024, 640), BF),
            V((16, 640, 256), BF), V((16, 640, 256), BF),
            V((4, 3, 4, 256, 256), BF), V((4, 3, 4, 256, 256), BF),
            V((4, 3, 256, 256), BF), V((4, 3, 256, 256), BF),
            V((4, 4, 256, 256), F32), V((4, 256, 256), F32),
            V((64, 8, CUT), BF), V((8, 8, 8, CUT), BF), V((8, 8, 8, CUT), BF),
            V((64, 8, 640 - CUT), BF), V((8, 8, 8, 640 - CUT), BF), V((8, 8, 8, 640 - CUT), BF),
            V((64, 8, 256), BF), V((8, 8, 8, 256), BF), V((8, 8, 8, 256), BF),
            V((8, 128), jnp.int32), V((8, 8, 128), jnp.int32), pltpu.SMEM((8, 8, 128), jnp.int32),
            V((32, 16, 128), BF), V((32, 16, 128), BF), V((16, 128), BF), V((32, 16, 128), BF),
            D((4,)), D, D((4,)), D((5,)), D, D((5,)),
            D((4, DEPTH)), D((2, 4, 4)), D, D((2, 4)), D((7,)), D((7,)), D((2,)), D((2,)), D,
            pltpu.SemaphoreType.REGULAR((4,)), pltpu.SemaphoreType.REGULAR((3,)),
        ],
        compiler_params=pltpu.CompilerParams(
            collective_id=0, has_side_effects=True, vmem_limit_bytes=60 * 2**20
        ),
    )(hidden, down_weight, down, up, row_tile_adapter, adapter_pool_slot)


def solution(mesh):
    placed = (
        P("grp", "tp"), P("tp", None), P("grp", None, "tp"), P("grp", None, "tp"), P("grp"), P(),
    )
    return jax.shard_map(local, mesh=mesh, in_specs=placed, out_specs=P("grp", "tp"), check_vma=False)
```

time: 75.3 us -> 66.3 us (0.88)
  Pallas kernels: 73.3 us -> 64.3 us
    pallas_call x1, Pallas kernels: 73.3 us -> 64.3 us  [local(): pl.pallas_call(kernel, out_shape=jax.ShapeDtypeStruct((1024, 256), BF), i...]
where the time goes in v3:
time: 66.3 us; the launch traced here: 66.2 us
  Pallas kernels  64.3 us (97%)
  local copies, waits for them, and re-layouts  1.87 us (3%)
    pallas_call x1, Pallas kernels, local(): pl.pallas_call(kernel, out_shape=jax.ShapeDtypeStruct((1024, 256), BF), i...  64.3 us
    unnamed x1, local copies, waits for them, and re-layouts  1.87 us

profile of v3, /device:TPU:1, one launch (start us, length us, event | category | flops | bytes accessed | tf_op | source)
XLA Modules:
  0.0 66.2 jit_solution(11811167057960004258)
XLA Ops:
  0.0 64.3 %shard_map.64 = bf16[1024,256]{1,0:T(8,128)(2,1)} custom-call(bf16[1024,640]{1,0:T(8,128)(2,1)} %hid.1, bf16[640,8192]{1,0:T(8,128)(2,1)} %wgt.1, bf16[8,8,8,640]{3,2,1,0:T(8,128)(2,1)} %bitcast.2, bf16[8,8,8,256]{3,2,1,0:T(8,128)(2,1)} %bitcast.3, s32[8]{0:T(128)} %tiles.1, s32[64]{0:T(128)} %slots.1), custom_call_target="tpu_custom_call" | custom-call | tf_op jit(solution)/shard_map/pallas_call | solution.py:431
  64.3 1.9 %copy.8 = bf16[1024,256]{1,0:T(8,128)(2,1)} copy(bf16[1024,256]{1,0:T(8,128)(2,1)} %shard_map.64) | data formatting | bytes 1048576

commit v4 on v3

v4 whole, which is shorter than its diff:
```python
import jax
import jax.numpy as jnp
from jax import lax
from jax.experimental import pallas as pl
from jax.experimental.pallas import tpu as pltpu
from jax.sharding import PartitionSpec as P

adapter_scale = 2.0
MESH = pl.DeviceIdType.MESH
NX, NY, NZ, NTP = 4, 4, 8, 32
BF, F32 = jnp.bfloat16, jnp.float32
CUT = 384
GROUPS = (
    ((2, 2),), ((2, 1), (1, 2)), ((2, 3), (3, 2)), ((2, 0), (0, 2)),
    ((1, 1), (1, 3), (3, 1), (3, 3), (1, 0), (3, 0), (0, 1), (0, 3), (0, 0)),
)


def kernel(
    hid, wgt, down, up, tiles, slots, out,
    h_own, h_sib, w_own, w_sib, send1, recv1, send2, recv2, part, hold,
    p_da, s_da, a_da, p_db, s_db, a_db, p_up, s_up, a_up, slot_out, slot_in, slot_s,
    rank_out, rank_in, rank_sum, rank_all, delta,
    h_l, h_s, h_r, w_l, w_s, w_r, s1_s, s1_r, s2_s, s2_r, z_s, z_r, r_s, r_r, loc_sem,
    ready_p, ready_z,
):
    z = lax.axis_index("grp")
    t = lax.axis_index("tp")
    core = lax.rem(t, 2)
    y = lax.rem(t // 2, NY)
    x = t // (2 * NY)

    def at(xx, yy, cc):
        return {"grp": z, "tp": (lax.rem(xx, NX) * NY + lax.rem(yy, NY)) * 2 + cc}

    def at_z(zz):
        return {"grp": zz, "tp": t}

    def at_t(tt):
        return {"grp": z, "tp": tt}

    def remote(src, dst, ssem, rsem, dev):
        return pltpu.make_async_remote_copy(
            src_ref=src, dst_ref=dst, send_sem=ssem, recv_sem=rsem,
            device_id=dev, device_id_type=MESH,
        )

    def got(ref, sem):
        pltpu.make_async_copy(ref, ref, sem).wait()

    sib = at(x, y, 1 - core)

    def blk(ox, oy):
        return lax.rem(x + ox, NX) * NY + lax.rem(y + oy, NY)

    def load_h(q):
        r = pl.ds(q * 256, 256)
        return pltpu.make_async_copy(hid.at[r], h_own.at[r], h_l.at[q])

    def load_w(b, g):
        c = pl.multiple_of((2 * b + core) * 256, 256)
        return pltpu.make_async_copy(wgt.at[:, pl.ds(c, 256)], w_own.at[b], w_l.at[g])

    def swap_h(q):
        r = pl.ds(q * 256, 256)
        return remote(hid.at[r], h_sib.at[r], h_s, h_r.at[q], sib)

    def swap_w(b, g):
        c = pl.multiple_of((2 * b + 1 - core) * 256, 256)
        return remote(wgt.at[:, pl.ds(c, 256)], w_sib.at[b], w_s, w_r.at[g], sib)

    barrier = pltpu.get_barrier_semaphore()
    near_plane = [sib] + [at(x + d, y, core) for d in (1, 3)] + [at(x, y + d, core) for d in (1, 3)]
    near_z = [at_z(lax.rem(z + d, NZ)) for d in (1, NZ - 1)]

    def tell(sem, devices):
        for dev in devices:
            pl.semaphore_signal(sem, inc=1, device_id=dev, device_id_type=MESH)

    tell(barrier, near_plane + near_z)
    for q in range(4):
        load_h(q).start()
    for g, group in enumerate(GROUPS):
        for ox, oy in group:
            load_w(blk(ox, oy), g).start()

    row = lax.broadcasted_iota(jnp.int32, (8, 128), 0)
    mine = jnp.zeros((8, 128), jnp.int32)
    for i in range(8):
        mine = jnp.where(row == i, slots[tiles[i]], mine)
    slot_out[...] = mine

    pl.semaphore_wait(barrier, 7)

    def hear_plane(k):
        pl.semaphore_wait(ready_p.at[k], 5)

    def hear_z(k):
        pl.semaphore_wait(ready_z.at[k], 2)

    LA, LB = pl.ds(0, CUT), pl.ds(CUT, 640 - CUT)

    def ends(n, p):
        mine_at = pl.ds(z * 8, 8)
        return (
            (slot_out, slot_in.at[z]),
            (down.at[:, p, :, LA], p_da.at[mine_at]),
            (down.at[:, p, :, LB], p_db.at[mine_at]),
            (up.at[:, p], p_up.at[mine_at]),
            (s_da.at[2 * p + core], a_da.at[:, 0, z]),
            (s_db.at[2 * p + core], a_db.at[:, 0, z]),
            (s_up.at[p], a_up.at[:, z]),
        )[n]

    whole = (slot_in, p_da, p_db, p_up, a_da, a_db, a_up)
    others = (
        slot_in.at[pl.ds(0, 7)], p_da.at[pl.ds(0, 56)], p_db.at[pl.ds(0, 56)], p_up.at[pl.ds(0, 56)],
        s_da.at[pl.ds(0, 15)], s_db.at[pl.ds(0, 15)], s_up.at[pl.ds(0, 7)],
    )

    def z_send(n, p):
        src, dst = ends(n, p)
        remote(src, dst, z_s.at[n], z_r.at[n], at_z(p)).start()

    def z_keep(n):
        src, dst = ends(n, z)
        pltpu.make_async_copy(src, dst, z_r.at[n]).start()

    def z_cross(n, p):
        src = (s_da if n == 4 else s_db).at[2 * p + 1 - core]
        dst = (a_da if n == 4 else a_db).at[:, 1, z]
        dev = {"grp": p, "tp": t + 1 - 2 * core}
        remote(src, dst, z_s.at[n], z_r.at[n], dev).start()

    def z_got(n):
        got(whole[n], z_r.at[n])

    def z_sent(n):
        got(others[n], z_s.at[n])

    def ring_z(d):
        return [lax.rem(z + dd, NZ) for dd in ((d, NZ - d) if d < NZ // 2 else (d,))]

    def start1(d, which):
        for n in which:
            for p in ring_z(d):
                z_send(n, p)

    tell(ready_z.at[0], near_z)
    swap_h(0).start()
    swap_w(blk(2, 2), 0).start()
    for q in range(1, 4):
        swap_h(q).start()
    start1(1, (0, 1, 2))
    for g in (1, 2, 3):
        for ox, oy in GROUPS[g]:
            swap_w(blk(ox, oy), g).start()
    tell(ready_p.at[0], near_plane)
    for n in (0, 1, 2, 3):
        z_keep(n)
    hear_z(0)
    tell(ready_z.at[1], near_z)
    start1(2, (0, 1))
    for ox, oy in GROUPS[4]:
        swap_w(blk(ox, oy), 4).start()

    def product(q, b):
        r = pl.ds(pl.multiple_of(q * 256, 256), 256)
        return jnp.dot(h_own[r, :], w_own[b], preferred_element_type=F32) + jnp.dot(
            h_sib[r, :], w_sib[b], preferred_element_type=F32
        )

    def order(j):
        return jnp.where(j == 0, 2, jnp.where(j == 1, 1, jnp.where(j == 2, 3, 0)))

    def block_of(f, along, across):
        first = f // 2 == 0
        return blk(jnp.where(first, along, across), jnp.where(first, across, along))

    def ahead(f):
        return jnp.where(lax.rem(f, 2) == 0, 1, 3)

    def other(f):
        return f + 1 - 2 * lax.rem(f, 2)

    def peer1(f):
        first = f // 2 == 0
        d = ahead(f)
        return at(x + jnp.where(first, d, 0), y + jnp.where(first, 0, d), core)

    def peer2(f):
        first = f // 2 == 0
        d = ahead(f)
        return at(x + jnp.where(first, 0, d), y + jnp.where(first, d, 0), core)

    def send_1(f, s, j):
        rsem = s1_r.at[0 if s == 0 else 1, j]
        remote(send1.at[f, s, j], recv1.at[f, s, j], s1_s, rsem, peer1(f)).start()

    def send_2(f, s):
        rsem = s2_r.at[4] if s == 0 else s2_r.at[other(f) if s == 1 else f]
        remote(send2.at[f, s], recv2.at[f, s], s2_s, rsem, peer2(f)).start()

    def need_w(g, n):
        got(w_own.at[pl.ds(0, n)], w_l.at[g])
        got(w_sib.at[pl.ds(0, n)], w_r.at[g])

    def step0(i, _):
        j = i // 4
        f = lax.rem(i, 4)

        @pl.when(j == 0)
        def _():
            got(h_own.at[pl.ds(0, 256)], h_l.at[f])
            got(h_sib.at[pl.ds(0, 256)], h_r.at[f])

        @pl.when(i == 0)
        def _():
            need_w(0, 1)

        @pl.when((f == 0) & (j > 0))
        def _():
            need_w(j, 2)

        send1[f, 0, j] = product(f, block_of(f, 2, order(j))).astype(BF)
        send_1(f, 0, j)
        return 0

    lax.fori_loop(0, 3, step0, 0)
    hear_z(1)
    tell(ready_z.at[2], near_z)
    start1(3, (0, 1))
    lax.fori_loop(3, 6, step0, 0)
    hear_z(2)
    start1(4, (0, 1))
    start1(2, (2,))
    start1(3, (2,))
    start1(4, (2,))
    lax.fori_loop(6, 16, step0, 0)
    hear_plane(0)
    tell(ready_p.at[1], near_plane)
    need_w(4, 9)

    def near1(i, _):
        j = i // 4
        f = lax.rem(i, 4)
        send1[f, 1, j] = product(other(f), block_of(f, ahead(f), order(j))).astype(BF)
        send_1(f, 1, j)
        return 0

    def near2(i, _):
        j = i // 4
        f = lax.rem(i, 4)
        v = product(f, block_of(f, ahead(f), order(j)))
        @pl.when(f == 0)
        def _():
            got(recv1.at[:, 0, j], s1_r.at[0, j])

        send1[f, 2, j] = (v + recv1[f, 0, j].astype(F32)).astype(BF)
        send_1(f, 2, j)
        return 0

    def step3(i, _):
        j = i // 4
        f = lax.rem(i, 4)
        part[f, j] = product(f, block_of(f, 0, order(j)))
        return 0

    def total1(q, j):
        @pl.when(q == 0)
        def _():
            got(recv1.at[:, pl.ds(1, 2), j], s1_r.at[1, j])

        return part[q, j] + recv1[q, 2, j].astype(F32) + recv1[other(q), 1, j].astype(F32)

    def turn0(q, _):
        send2[q, 0] = total1(q, 0).astype(BF)
        send_2(q, 0)
        return 0

    def turn1(i, _):
        j = 1 + i // 4
        q = lax.rem(i, 4)
        v = total1(q, j)
        keep = lax.rem(q, 2) == j - 1

        @pl.when(keep)
        def _():
            hold[q] = v

        @pl.when(jnp.logical_not(keep))
        def _():
            send2[other(q), 1] = v.astype(BF)
            send_2(other(q), 1)

        return 0

    def turn2(q, _):
        v = hold[q]
        @pl.when(q == 0)
        def _():
            got(recv2.at[:, 0], s2_r.at[4])

        send2[q, 2] = (v + recv2[q, 0].astype(F32)).astype(BF)
        send_2(q, 2)
        return 0

    def turn3(q, _):
        part[q, 3] = total1(q, 3)
        return 0

    def pick(n, src, dst):
        def one(p):
            def body(i, _):
                v = src[slot_s[p, i, 0]]
                if n == 6:
                    dst[p, i] = v
                else:
                    dst[2 * p + lax.rem(i, 2), i // 2] = v
                return 0
            lax.fori_loop(0, 8, body, 0)

        def send(i, _):
            p = lax.rem(z + i, NZ)
            one(p)
            z_send(n, p)
            if n != 6:
                z_cross(n, p)
            return 0

        lax.fori_loop(1, NZ, send, 0)
        one(z)
        z_keep(n)
        if n != 6:
            z_cross(n, z)

    lax.fori_loop(0, 4, near1, 0)
    z_got(0)
    cp = pltpu.make_async_copy(slot_in, slot_s, loc_sem)
    cp.start()
    hear_plane(1)
    tell(ready_p.at[2], near_plane)
    lax.fori_loop(0, 4, near2, 0)
    cp.wait()
    z_got(1)
    pick(4, p_da, s_da)
    lax.fori_loop(4, 8, near1, 0)
    lax.fori_loop(4, 8, near2, 0)
    z_got(2)
    pick(5, p_db, s_db)

    def start_up(i, _):
        z_send(3, lax.rem(z + i, NZ))
        return 0

    lax.fori_loop(1, NZ, start_up, 0)
    lax.fori_loop(8, 12, near1, 0)
    lax.fori_loop(8, 12, near2, 0)
    hear_plane(2)
    tell(ready_p.at[3], near_plane)
    lax.fori_loop(0, 4, step3, 0)
    lax.fori_loop(0, 4, turn0, 0)
    lax.fori_loop(4, 8, step3, 0)
    lax.fori_loop(0, 4, turn1, 0)
    hear_plane(3)
    lax.fori_loop(8, 16, step3, 0)

    z_got(4)
    z_got(5)
    nt = (((1,), (1,)), ((), ()))
    for m in range(4):
        r = pl.ds(pl.multiple_of((2 * m + core) * 128, 128), 128)
        v = jnp.zeros((64, 128), F32)
        for k, h in ((0, h_own), (1, h_sib)):
            v += lax.dot_general(
                a_da[m, k].reshape(64, CUT), h[r, 0:CUT], nt, preferred_element_type=F32
            ) + lax.dot_general(
                a_db[m, k].reshape(64, 640 - CUT), h[r, CUT:640], nt, preferred_element_type=F32
            )
        rank_out[pl.ds(m * 4, 4)] = v.astype(BF).reshape(4, 16, 128)

    chip = t // 2

    def send_a(i, _):
        p = lax.rem(chip + i, 16)
        remote(rank_out.at[p], rank_in.at[chip], r_s.at[0], r_r.at[0], at_t(2 * p + core)).start()
        return 0

    def send_b(i, _):
        p = lax.rem(chip + i, 16)
        remote(rank_sum, rank_all.at[0, chip], r_s.at[1], r_r.at[1], at_t(2 * p + core)).start()
        return 0

    lax.fori_loop(1, 16, send_a, 0)
    pltpu.make_async_copy(rank_out.at[chip], rank_in.at[chip], r_r.at[0]).start()
    lax.fori_loop(12, 16, near1, 0)
    lax.fori_loop(12, 16, near2, 0)
    z_got(3)
    pick(6, p_up, s_up)
    lax.fori_loop(4, 8, turn1, 0)
    got(rank_in, r_r.at[0])

    def add_rank(i, acc):
        return acc + rank_in[i].astype(F32)

    rank_sum[...] = lax.fori_loop(0, 16, add_rank, jnp.zeros((16, 128), F32)).astype(BF)
    lax.fori_loop(1, 16, send_b, 0)
    pltpu.make_async_copy(rank_sum, rank_all.at[0, chip], r_r.at[1]).start()
    lax.fori_loop(0, 4, turn2, 0)

    got(h_sib, h_s)
    got(w_sib, w_s)
    for n in range(6):
        z_sent(n)
    lax.fori_loop(0, 4, turn3, 0)

    got(rank_all.at[0], r_r.at[1])
    remote(rank_all.at[0], rank_all.at[1], r_s.at[2], r_r.at[2], sib).start()
    z_got(6)

    def adapt(half):
        for m in range(4):
            i = 2 * m + (core if half == 0 else 1 - core)
            v = lax.dot_general(
                rank_all[half, m * 4:m * 4 + 4].reshape(64, 128), a_up[i].reshape(64, 256),
                (((0,), (0,)), ((), ())), preferred_element_type=F32,
            )
            r = pl.ds(pl.multiple_of(lax.rem(i, 2) * 128, 128), 128)
            delta[m, r, :] = (v * adapter_scale).astype(BF).astype(F32)

    adapt(0)
    got(rank_all.at[1], r_r.at[2])
    adapt(1)
    got(send1, s1_s)
    got(rank_in.at[pl.ds(0, 15)], r_s.at[0])
    got(rank_in.at[pl.ds(0, 15)], r_s.at[1])
    got(rank_all.at[0], r_s.at[2])
    z_sent(6)

    def last(q, _):
        got(recv2.at[q, pl.ds(1, 2)], s2_r.at[q])
        v = part[q, 3] + recv2[q, 2].astype(F32) + recv2[other(q), 1].astype(F32) + delta[q]
        out[pl.ds(pl.multiple_of(q * 256, 256), 256), :] = v.astype(BF)
        return 0

    lax.fori_loop(0, 4, last, 0)
    got(send2, s2_s)


def local(hidden, down_weight, adapter_down_factor, adapter_up_factor, row_tile_adapter, adapter_pool_slot):
    any_ = pl.BlockSpec(memory_space=pl.ANY)
    smem = pl.BlockSpec(memory_space=pltpu.SMEM)
    V, D = pltpu.VMEM, pltpu.SemaphoreType.DMA
    down = adapter_down_factor.reshape(8, 8, 8, 640)
    up = adapter_up_factor.reshape(8, 8, 8, 256)
    return pl.pallas_call(
        kernel,
        out_shape=pltpu.VMEM((1024, 256), BF),
        in_specs=[any_, any_, any_, any_, smem, smem],
        out_specs=pl.BlockSpec(memory_space=pltpu.VMEM),
        scratch_shapes=[
            V((1024, 640), BF), V((1024, 640), BF),
            V((16, 640, 256), BF), V((16, 640, 256), BF),
            V((4, 3, 4, 256, 256), BF), V((4, 3, 4, 256, 256), BF),
            V((4, 3, 256, 256), BF), V((4, 3, 256, 256), BF),
            V((4, 4, 256, 256), F32), V((4, 256, 256), F32),
            V((64, 8, CUT), BF), V((16, 4, 8, CUT), BF), V((4, 2, 8, 8, CUT), BF),
            V((64, 8, 640 - CUT), BF), V((16, 4, 8, 640 - CUT), BF), V((4, 2, 8, 8, 640 - CUT), BF),
            V((64, 8, 256), BF), V((8, 8, 8, 256), BF), V((8, 8, 8, 256), BF),
            V((8, 128), jnp.int32), V((8, 8, 128), jnp.int32), pltpu.SMEM((8, 8, 128), jnp.int32),
            V((16, 16, 128), BF), V((16, 16, 128), BF), V((16, 128), BF), V((2, 16, 16, 128), BF), V((4, 256, 256), F32),
            D((4,)), D, D((4,)), D((5,)), D, D((5,)),
            D, D((2, 4)), D, D((5,)), D((7,)), D((7,)), D((3,)), D((3,)), D,
            pltpu.SemaphoreType.REGULAR((4,)), pltpu.SemaphoreType.REGULAR((3,)),
        ],
        compiler_params=pltpu.CompilerParams(
            collective_id=0, has_side_effects=True, vmem_limit_bytes=60 * 2**20
        ),
    )(hidden, down_weight, down, up, row_tile_adapter, adapter_pool_slot)


def solution(mesh):
    placed = (
        P("grp", "tp"), P("tp", None), P("grp", None, "tp"), P("grp", None, "tp"), P("grp"), P(),
    )
    return jax.shard_map(local, mesh=mesh, in_specs=placed, out_specs=P("grp", "tp"), check_vma=False)
```

time: 66.3 us -> 60.7 us (0.916)
  Pallas kernels: 64.3 us -> 59.8 us
  local copies, waits for them, and re-layouts: 1.87 us -> 0.8 us
    pallas_call x1, Pallas kernels: 64.3 us -> 59.8 us  [local(): pl.pallas_call(kernel, out_shape=pltpu.VMEM((1024, 256), BF), in_specs=[a...]
    unnamed x1, local copies, waits for them, and re-layouts: 1.87 us -> 0.8 us
where the time goes in v4:
time: 60.7 us; the launch traced here: 60.6 us
  Pallas kernels  59.8 us (99%)
  local copies, waits for them, and re-layouts  0.8 us (1%)
    pallas_call x1, Pallas kernels, local(): pl.pallas_call(kernel, out_shape=pltpu.VMEM((1024, 256), BF), in_specs=[a...  59.8 us

profile of v4, /device:TPU:1, one launch (start us, length us, event | category | flops | bytes accessed | tf_op | source)
XLA Modules:
  0.0 60.6 jit_solution(15237515585295360810)
XLA Ops:
  0.0 59.8 %shard_map.64 = bf16[1024,256]{1,0:T(8,128)(2,1)S(1)} custom-call(bf16[1024,640]{1,0:T(8,128)(2,1)} %hid.1, bf16[640,8192]{1,0:T(8,128)(2,1)} %wgt.1, bf16[8,8,8,640]{3,2,1,0:T(8,128)(2,1)} %bitcast.2, bf16[8,8,8,256]{3,2,1,0:T(8,128)(2,1)} %bitcast.3, s32[8]{0:T(128)} %tiles.1, s32[64]{0:T(128)} %slots.1), custom_call_target="tpu_custom_call" | custom-call | tf_op jit(solution)/shard_map/pallas_call | solution.py:456
  59.8 0.8 %copy.8 = bf16[1024,256]{1,0:T(8,128)(2,1)} copy(bf16[1024,256]{1,0:T(8,128)(2,1)S(1)} %shard_map.64) | data formatting | bytes 1048576

commit v5 on v4

--- a/solution.py
+++ b/solution.py
@@ -17,11 +17,11 @@
 
 
 def kernel(
-    hid, wgt, down, up, tiles, slots, out,
+    hid, wgt, down, up, tiles_any, slots_any, out, tiles, slots,
     h_own, h_sib, w_own, w_sib, send1, recv1, send2, recv2, part, hold,
     p_da, s_da, a_da, p_db, s_db, a_db, p_up, s_up, a_up, slot_out, slot_in, slot_s,
     rank_out, rank_in, rank_sum, rank_all, delta,
-    h_l, h_s, h_r, w_l, w_s, w_r, s1_s, s1_r, s2_s, s2_r, z_s, z_r, r_s, r_r, loc_sem,
+    h_l, h_s, h_r, w_l, w_s, w_r, s1_s, s1_r, s2_s, s2_r, z_s, z_r, r_s, r_r, loc_sem, t_sem,
     ready_p, ready_z,
 ):
     z = lax.axis_index("grp")
@@ -78,17 +78,17 @@
             pl.semaphore_signal(sem, inc=1, device_id=dev, device_id_type=MESH)
 
     tell(barrier, near_plane + near_z)
+    tables = [
+        pltpu.make_async_copy(tiles_any, tiles, t_sem.at[0]),
+        pltpu.make_async_copy(slots_any, slots, t_sem.at[1]),
+    ]
+    for cp in tables:
+        cp.start()
     for q in range(4):
         load_h(q).start()
     for g, group in enumerate(GROUPS):
         for ox, oy in group:
             load_w(blk(ox, oy), g).start()
-
-    row = lax.broadcasted_iota(jnp.int32, (8, 128), 0)
-    mine = jnp.zeros((8, 128), jnp.int32)
-    for i in range(8):
-        mine = jnp.where(row == i, slots[tiles[i]], mine)
-    slot_out[...] = mine
 
     pl.semaphore_wait(barrier, 7)
 
@@ -151,18 +151,26 @@
     swap_w(blk(2, 2), 0).start()
     for q in range(1, 4):
         swap_h(q).start()
-    start1(1, (0, 1, 2))
+    start1(1, (1, 2))
     for g in (1, 2, 3):
         for ox, oy in GROUPS[g]:
             swap_w(blk(ox, oy), g).start()
     tell(ready_p.at[0], near_plane)
-    for n in (0, 1, 2, 3):
+    for n in (1, 2, 3):
         z_keep(n)
+    for ox, oy in GROUPS[4]:
+        swap_w(blk(ox, oy), 4).start()
+
+    far = blk(2, 2)
+    got(w_own.at[0], w_l.at[0])
+    for f in range(4):
+        got(h_own.at[pl.ds(0, 256)], h_l.at[f])
+        part[f, 0] = jnp.dot(
+            h_own[f * 256:(f + 1) * 256, :], w_own[far], preferred_element_type=F32
+        )
     hear_z(0)
     tell(ready_z.at[1], near_z)
-    start1(2, (0, 1))
-    for ox, oy in GROUPS[4]:
-        swap_w(blk(ox, oy), 4).start()
+    start1(2, (1,))
 
     def product(q, b):
         r = pl.ds(pl.multiple_of(q * 256, 256), 256)
@@ -205,20 +213,20 @@
         got(w_own.at[pl.ds(0, n)], w_l.at[g])
         got(w_sib.at[pl.ds(0, n)], w_r.at[g])
 
+    got(w_sib.at[0], w_r.at[0])
+    for f in range(4):
+        got(h_sib.at[pl.ds(0, 256)], h_r.at[f])
+        send1[f, 0, 0] = (
+            part[f, 0]
+            + jnp.dot(h_sib[f * 256:(f + 1) * 256, :], w_sib[far], preferred_element_type=F32)
+        ).astype(BF)
+        send_1(f, 0, 0)
+
     def step0(i, _):
         j = i // 4
         f = lax.rem(i, 4)
 
-        @pl.when(j == 0)
-        def _():
-            got(h_own.at[pl.ds(0, 256)], h_l.at[f])
-            got(h_sib.at[pl.ds(0, 256)], h_r.at[f])
-
-        @pl.when(i == 0)
-        def _():
-            need_w(0, 1)
-
-        @pl.when((f == 0) & (j > 0))
+        @pl.when(f == 0)
         def _():
             need_w(j, 2)
 
@@ -226,17 +234,27 @@
         send_1(f, 0, j)
         return 0
 
-    lax.fori_loop(0, 3, step0, 0)
     hear_z(1)
     tell(ready_z.at[2], near_z)
-    start1(3, (0, 1))
-    lax.fori_loop(3, 6, step0, 0)
+    for cp in tables:
+        cp.wait()
+    row = lax.broadcasted_iota(jnp.int32, (8, 128), 0)
+    mine = jnp.zeros((8, 128), jnp.int32)
+    for i in range(8):
+        mine = jnp.where(row == i, slots[tiles[i]], mine)
+    slot_out[...] = mine
+
+    z_keep(0)
+    start1(3, (1,))
+    lax.fori_loop(4, 7, step0, 0)
     hear_z(2)
-    start1(4, (0, 1))
+    for d in (4, 3, 2, 1):
+        start1(d, (0,))
+    start1(4, (1,))
     start1(2, (2,))
     start1(3, (2,))
     start1(4, (2,))
-    lax.fori_loop(6, 16, step0, 0)
+    lax.fori_loop(7, 16, step0, 0)
     hear_plane(0)
     tell(ready_p.at[1], near_plane)
     need_w(4, 9)
@@ -365,6 +383,14 @@
     hear_plane(3)
     lax.fori_loop(8, 16, step3, 0)
 
+    def near1_odd(i, _):
+        return near1(13 + 2 * i, 0)
+
+    def near1_even(i, _):
+        return near1(12 + 2 * i, 0)
+
+    lax.fori_loop(0, 2, near1_odd, 0)
+
     z_got(4)
     z_got(5)
     nt = (((1,), (1,)), ((), ()))
@@ -393,7 +419,7 @@
 
     lax.fori_loop(1, 16, send_a, 0)
     pltpu.make_async_copy(rank_out.at[chip], rank_in.at[chip], r_r.at[0]).start()
-    lax.fori_loop(12, 16, near1, 0)
+    lax.fori_loop(0, 2, near1_even, 0)
     lax.fori_loop(12, 16, near2, 0)
     z_got(3)
     pick(6, p_up, s_up)
@@ -431,34 +457,34 @@
     adapt(0)
     got(rank_all.at[1], r_r.at[2])
     adapt(1)
+
+    def last(q, _):
+        got(recv2.at[q, pl.ds(1, 2)], s2_r.at[q])
+        v = part[q, 3] + recv2[q, 2].astype(F32) + recv2[other(q), 1].astype(F32) + delta[q]
+        out[pl.ds(pl.multiple_of(q * 256, 256), 256), :] = v.astype(BF)
+        return 0
+
+    lax.fori_loop(0, 4, last, 0)
     got(send1, s1_s)
     got(rank_in.at[pl.ds(0, 15)], r_s.at[0])
     got(rank_in.at[pl.ds(0, 15)], r_s.at[1])
     got(rank_all.at[0], r_s.at[2])
     z_sent(6)
-
-    def last(q, _):
-        got(recv2.at[q, pl.ds(1, 2)], s2_r.at[q])
-        v = part[q, 3] + recv2[q, 2].astype(F32) + recv2[other(q), 1].astype(F32) + delta[q]
-        out[pl.ds(pl.multiple_of(q * 256, 256), 256), :] = v.astype(BF)
-        return 0
-
-    lax.fori_loop(0, 4, last, 0)
     got(send2, s2_s)
 
 
 def local(hidden, down_weight, adapter_down_factor, adapter_up_factor, row_tile_adapter, adapter_pool_slot):
     any_ = pl.BlockSpec(memory_space=pl.ANY)
-    smem = pl.BlockSpec(memory_space=pltpu.SMEM)
     V, D = pltpu.VMEM, pltpu.SemaphoreType.DMA
     down = adapter_down_factor.reshape(8, 8, 8, 640)
     up = adapter_up_factor.reshape(8, 8, 8, 256)
     return pl.pallas_call(
         kernel,
         out_shape=pltpu.VMEM((1024, 256), BF),
-        in_specs=[any_, any_, any_, any_, smem, smem],
+        in_specs=[any_] * 6,
         out_specs=pl.BlockSpec(memory_space=pltpu.VMEM),
         scratch_shapes=[
+            pltpu.SMEM((8,), jnp.int32), pltpu.SMEM((64,), jnp.int32),
             V((1024, 640), BF), V((1024, 640), BF),
             V((16, 640, 256), BF), V((16, 640, 256), BF),
             V((4, 3, 4, 256, 256), BF), V((4, 3, 4, 256, 256), BF),
@@ -470,7 +496,7 @@
             V((8, 128), jnp.int32), V((8, 8, 128), jnp.int32), pltpu.SMEM((8, 8, 128), jnp.int32),
             V((16, 16, 128), BF), V((16, 16, 128), BF), V((16, 128), BF), V((2, 16, 16, 128), BF), V((4, 256, 256), F32),
             D((4,)), D, D((4,)), D((5,)), D, D((5,)),
-            D, D((2, 4)), D, D((5,)), D((7,)), D((7,)), D((3,)), D((3,)), D,
+            D, D((2, 4)), D, D((5,)), D((7,)), D((7,)), D((3,)), D((3,)), D, D((2,)),
             pltpu.SemaphoreType.REGULAR((4,)), pltpu.SemaphoreType.REGULAR((3,)),
         ],
         compiler_params=pltpu.CompilerParams(

time: 60.7 us -> 60 us (0.988)
    pallas_call x1, Pallas kernels: 59.8 us -> 59.2 us  [local(): pl.pallas_call(kernel, out_shape=pltpu.VMEM((1024, 256), BF), in_specs=[a...]
where the time goes in v5:
time: 60 us
  Pallas kernels  59.2 us (99%)
  local copies, waits for them, and re-layouts  0.8 us (1%)
    pallas_call x1, Pallas kernels, local(): pl.pallas_call(kernel, out_shape=pltpu.VMEM((1024, 256), BF), in_specs=[a...  59.2 us

profile of v5, /device:TPU:1, one launch (start us, length us, event | category | flops | bytes accessed | tf_op | source)
XLA Modules:
  0.0 60.0 jit_solution(2990967299048553151)
XLA Ops:
  0.0 59.2 %shard_map.64 = bf16[1024,256]{1,0:T(8,128)(2,1)S(1)} custom-call(bf16[1024,640]{1,0:T(8,128)(2,1)} %hid.1, bf16[640,8192]{1,0:T(8,128)(2,1)} %wgt.1, bf16[8,8,8,640]{3,2,1,0:T(8,128)(2,1)} %bitcast.2, bf16[8,8,8,256]{3,2,1,0:T(8,128)(2,1)} %bitcast.3, s32[8]{0:T(128)} %tiles_any.1, s32[64]{0:T(128)} %slots_any.1), custom_call_target="tpu_custom_call" | custom-call | tf_op jit(solution)/shard_map/pallas_call | solution.py:481
  59.2 0.8 %copy.8 = bf16[1024,256]{1,0:T(8,128)(2,1)} copy(bf16[1024,256]{1,0:T(8,128)(2,1)S(1)} %shard_map.64) | data formatting | bytes 1048576

commit v6 on v5

--- a/solution.py
+++ b/solution.py
@@ -415,6 +415,7 @@
     def send_b(i, _):
         p = lax.rem(chip + i, 16)
         remote(rank_sum, rank_all.at[0, chip], r_s.at[1], r_r.at[1], at_t(2 * p + core)).start()
+        remote(rank_sum, rank_all.at[1, chip], r_s.at[2], r_r.at[2], at_t(2 * p + 1 - core)).start()
         return 0
 
     lax.fori_loop(1, 16, send_a, 0)
@@ -432,6 +433,7 @@
     rank_sum[...] = lax.fori_loop(0, 16, add_rank, jnp.zeros((16, 128), F32)).astype(BF)
     lax.fori_loop(1, 16, send_b, 0)
     pltpu.make_async_copy(rank_sum, rank_all.at[0, chip], r_r.at[1]).start()
+    remote(rank_sum, rank_all.at[1, chip], r_s.at[2], r_r.at[2], sib).start()
     lax.fori_loop(0, 4, turn2, 0)
 
     got(h_sib, h_s)
@@ -441,7 +443,6 @@
     lax.fori_loop(0, 4, turn3, 0)
 
     got(rank_all.at[0], r_r.at[1])
-    remote(rank_all.at[0], rank_all.at[1], r_s.at[2], r_r.at[2], sib).start()
     z_got(6)
 
     def adapt(half):

time: 60 us -> 59.7 us (level)
  no operation moved by 1% of the time
where the time goes in v6:
time: 59.7 us
  Pallas kernels  58.9 us (99%)
  local copies, waits for them, and re-layouts  0.8 us (1%)
    pallas_call x1, Pallas kernels, local(): pl.pallas_call(kernel, out_shape=pltpu.VMEM((1024, 256), BF), in_specs=[a...  58.9 us

profile of v6, /device:TPU:1, one launch (start us, length us, event | category | flops | bytes accessed | tf_op | source)
XLA Modules:
  0.0 59.7 jit_solution(17057067881412129111)
XLA Ops:
  0.0 58.9 %shard_map.64 = bf16[1024,256]{1,0:T(8,128)(2,1)S(1)} custom-call(bf16[1024,640]{1,0:T(8,128)(2,1)} %hid.1, bf16[640,8192]{1,0:T(8,128)(2,1)} %wgt.1, bf16[8,8,8,640]{3,2,1,0:T(8,128)(2,1)} %bitcast.2, bf16[8,8,8,256]{3,2,1,0:T(8,128)(2,1)} %bitcast.3, s32[8]{0:T(128)} %tiles_any.1, s32[64]{0:T(128)} %slots_any.1), custom_call_target="tpu_custom_call" | custom-call | tf_op jit(solution)/shard_map/pallas_call | solution.py:482
  58.9 0.8 %copy.8 = bf16[1024,256]{1,0:T(8,128)(2,1)} copy(bf16[1024,256]{1,0:T(8,128)(2,1)S(1)} %shard_map.64) | data formatting | bytes 1048576
